TPU v7x, 128 devices: a whole 4x4x4 slice. The times are simulated.
128 devices in a mesh: dp: 16 (over z, y), expert: 8 (over x, core).
Axes of the slice: x: 4, y: 4, z: 4, core: 2. Of those that a mesh axis runs over, the one named last changes fastest.
Arguments:
- hidden: bfloat16 [8, 1024, 8192], P('expert', None, 'dp'), may hold values from -6 to 6
- down_weight: bfloat16 [8, 8192, 6144], P('expert', 'dp'), may hold values from -0.0625 to 0.0625
- grad_out: bfloat16 [2048, 6144], P('dp', 'expert'), may hold values from -2 to 2
- routing: int32 [2048, 2], P('dp'), may hold values from 0 to 7, all different within a row; in each aligned block of 128 rows (0 to 127, 128 to 255, ...) at most 64 rows name the same one
- gates: float32 [2048, 2], P('dp'), may hold values from 0.25 to 1
Outputs:
- mixed_out: bfloat16 [2048, 6144], P('dp', 'expert')
- grad_hidden: bfloat16 [8, 1024, 8192], P('expert', None, 'dp')
- grad_weight: bfloat16 [8, 8192, 6144], P('expert', 'dp')
Inputs may be any that keep to these rules, and one draw needn't show every extreme that they name: `routing`: among the 128 tokens of one sequence shard (aligned blocks of rows), each expert is named by at most 64 tokens, a bound that some block reaches; a token names 2 different experts.
All inputs are finite; a program needn't handle non-finite values.
Results may differ from a plain program's by a relative error of at most 0.017.
Values may be sent and summed in bfloat16 or wider, within the bound.
A program may use at most 128 MiB of HBM per device.

v0:
```python
import jax
import jax.numpy as jnp
from jax import lax
from jax.sharding import PartitionSpec as P


def dispatch_weights(routing, gates, experts, capacity):
    flattened = routing.reshape(-1)
    onehot = (flattened[:, None] == jnp.arange(experts, dtype=jnp.int32)[None, :]).astype(jnp.int32)
    position = jnp.sum((jnp.cumsum(onehot, axis=0) - onehot) * onehot, axis=1)
    target = flattened * capacity + position
    picked = (jnp.arange(experts * capacity, dtype=jnp.int32)[:, None] == target[None, :]).astype(
        jnp.float32
    )
    picked = picked * gates.reshape(-1)[None, :]
    return jnp.sum(picked.reshape(experts * capacity, routing.shape[0], routing.shape[1]), axis=2)


def body(hidden, down_weight, grad_out, routing, gates):
    highest = lax.Precision.HIGHEST
    groups = lax.axis_size("dp")
    owners = lax.axis_size("expert")
    experts = hidden.shape[0] * owners
    slot_total = hidden.shape[1]
    capacity = slot_total // groups
    dispatch = dispatch_weights(routing, gates, experts, capacity)
    hidden_rows = hidden[0]
    weight = down_weight[0]
    own_rows = lax.psum_scatter(
        jnp.dot(hidden_rows, weight, preferred_element_type=jnp.float32).astype(jnp.bfloat16),
        "dp",
        scatter_dimension=0,
        tiled=True,
    ).astype(jnp.float32)
    own_rows = own_rows.astype(jnp.bfloat16)[None]
    outputs = lax.all_to_all(own_rows, "expert", split_axis=2, concat_axis=0, tiled=True)
    flat_outputs = outputs.reshape(experts * capacity, outputs.shape[-1]).astype(jnp.float32)
    mixed_out = lax.dot_general(dispatch, flat_outputs, (((0,), (0,)), ((), ())), precision=highest)
    mixed_out = mixed_out.astype(jnp.bfloat16)
    routed = jnp.dot(dispatch, grad_out.astype(jnp.float32), precision=highest).astype(jnp.bfloat16)
    routed = routed.reshape(experts, capacity, routed.shape[-1])
    shards = lax.all_gather(routed, "dp", axis=1, tiled=True)
    gathered = lax.all_to_all(shards, "expert", split_axis=0, concat_axis=2, tiled=True)
    grad_rows = gathered[0]
    hidden_acc = lax.dot_general(
        grad_rows, weight, (((1,), (1,)), ((), ())), preferred_element_type=jnp.float32
    )
    weight_acc = lax.dot_general(
        hidden_rows, grad_rows, (((0,), (0,)), ((), ())), preferred_element_type=jnp.float32
    )
    grad_hidden = hidden_acc.astype(jnp.bfloat16)[None]
    grad_weight = weight_acc.astype(jnp.bfloat16)[None]
    return (mixed_out, grad_hidden, grad_weight)


def solution(mesh):
    return jax.shard_map(
        body,
        mesh=mesh,
        in_specs=(
            P("expert", None, "dp"),
            P("expert", "dp", None),
            P("dp", "expert"),
            P("dp", None),
            P("dp", None),
        ),
        out_specs=(P("dp", "expert"), P("expert", None, "dp"), P("expert", "dp", None)),
        check_vma=False,
    )
```

profile of v0, /device:TPU:1, one launch (start us, length us, event | category | flops | bytes accessed | tf_op | source)
XLA Modules:
  0.0 412.6 jit_solution(2753633807053152809)
XLA Ops:
  7.2 0.0 copy-start
  7.2 0.0 reduce-scatter.2.cloned.1.call-start
  7.2 1.2 copy-done
  8.4 12.3 %convolution_convert_fusion = bf16[1024,6144]{1,0:T(8,128)(2,1)} fusion(bf16[1,512,6144]{2,1,0:T(8,128)(2,1)} %param.6, bf16[1,1024,512]{2,1,0:T(8,128)(2,1)S(1)} %copy-done), kind=kOutput, calls=%fused_computation | convolution fusion | flops 6448742400 | bytes 19922944 | tf_op jit(solution)/shard_map/dot_general | solution.py:30
  20.7 0.0 copy-start.2
  20.7 0.0 copy-start.3
  20.7 0.0 copy-start.1
  20.7 0.0 reduce-scatter.2.cloned.1.call-update
  20.7 0.0 all-gather.2.cloned.1.call-start
  20.7 0.6 copy-done.2
  21.3 0.1 copy.50
  21.5 0.1 eq.44
  21.6 0.1 eq.40
  21.8 0.6 reduce-window.6
  22.3 0.2 slice_reduce_fusion
  22.6 0.1 fusion.13
  22.7 0.1 reduce_sum.21
  22.8 0.1 copy.52
  22.9 0.0 copy-done.3
  22.9 0.1 select_reduce_fusion
  23.0 0.0 copy-done.1
  23.0 0.8 convolution_convert_fusion.2
  23.8 1.3 copy.56
  25.1 0.0 all-gather.2.cloned.1.call-update
  25.1 93.8 %reduce-scatter.2.cloned.1.call-done = bf16[64,6144]{1,0:T(8,128)(2,1)} async-done(((bf16[1024,6144]{1,0:T(8,128)(2,1)}), bf16[64,6144]{1,0:T(8,128)(2,1)}) %reduce-scatter.2.cloned.1.call-update) | async-done | bytes 786448 | tf_op jit(solution)/shard_map/reduce_scatter | solution.py:29
  118.9 7.2 %copy.53 = bf16[1,64,6144]{1,0,2:T(2,128)(2,1)} copy(bf16[1,64,6144]{2,1,0:T(8,128)(2,1)} %bitcast.58) | data formatting | bytes 1572864 | tf_op jit(solution)/shard_map/broadcast_in_dim | solution.py:35
  126.1 0.5 broadcast.37
  126.6 34.3 %reduce.2 = bf16[6144,64]{1,0:T(8,128)(2,1)S(1)} reduce(bf16[6144,1,64]{2,1,0:T(2,128)(2,1)} %bitcast.52, bf16[]{:T(256)} %broadcast.37), dimensions={1}, to_apply=%bitcast.43.reduce_sub_computation | reduce | bytes 1572866
  161.0 1.9 reshape.59
  162.9 5.4 %all-to-all-start = ((bf16[8,2,24576]{2,1,0:T(2,128)(2,1)}), bf16[8,2,24576]{2,1,0:T(2,128)(2,1)S(1)}, u32[]{:S(2)}, u32[]{:S(2)}) async-start(bf16[8,2,24576]{2,1,0:T(2,128)(2,1)} %reshape.59), calls=%async_computation.1 | async-start | bytes 1572864 | tf_op jit(solution)/shard_map/all_to_all | solution.py:36
  168.3 41.9 %all-gather.2.cloned.1.call-done = bf16[8,1024,768]{2,0,1:T(8,128)(2,1)} async-done(((bf16[8,64,768]{2,0,1:T(8,128)(2,1)}), bf16[8,1024,768]{2,0,1:T(8,128)(2,1)}) %all-gather.2.cloned.1.call-update) | async-done | bytes 12582928 | tf_op jit(solution)/shard_map/all_gather | solution.py:42
  210.2 16.5 %copy.57 = bf16[8,1024,768]{1,2,0:T(8,128)(2,1)} copy(bf16[8,1024,768]{2,0,1:T(8,128)(2,1)} %all-gather.2.cloned.1.call-done) | data formatting | bytes 25165824 | tf_op jit(solution)/shard_map/all_gather | solution.py:42
  226.7 0.0 all-to-all-done
  226.7 6.2 %all-to-all-start.1 = ((bf16[8,1024,768]{1,2,0:T(8,128)(2,1)}), bf16[8,1024,768]{1,2,0:T(8,128)(2,1)}, u32[]{:S(2)}, u32[]{:S(2)}) async-start(bf16[8,1024,768]{1,2,0:T(8,128)(2,1)} %copy.57), calls=%async_computation.2 | async-start | bytes 25165824 | tf_op jit(solution)/shard_map/all_to_all | solution.py:43
  232.9 3.9 reshape.60
  236.9 6.0 %copy.54 = bf16[1,64,6144]{2,1,0:T(8,128)(2,1)S(1)} copy(bf16[1,64,6144]{1,0,2:T(2,128)(2,1)} %bitcast.53) | data formatting | bytes 1572864 | tf_op jit(solution)/shard_map/all_to_all | solution.py:36
  242.9 0.1 copy.59
  243.1 0.1 bitcast_bitcast_fusion
  243.1 0.1 copy.55
  243.3 1.2 convolution_convert_fusion.3
  244.5 127.1 %all-to-all-done.1 = bf16[8,1024,768]{1,2,0:T(8,128)(2,1)} async-done(((bf16[8,1024,768]{1,2,0:T(8,128)(2,1)}), bf16[8,1024,768]{1,2,0:T(8,128)(2,1)}, u32[]{:S(2)}, u32[]{:S(2)}) %all-to-all-start.1) | async-done | bytes 12582944 | tf_op jit(solution)/shard_map/all_to_all | solution.py:43
  371.6 12.4 %fusion.7 = bf16[1,1024,512]{2,1,0:T(8,128)(2,1)} fusion(bf16[1024,6144]{0,1:T(8,128)(2,1)} %bitcast.10, bf16[1,512,6144]{2,1,0:T(8,128)(2,1)} %param.6), kind=kOutput, calls=%fused_computation.8 | convolution fusion | flops 6442975232 | bytes 19922944 | tf_op jit(solution)/shard_map/dot_general | solution.py:45
  384.0 13.1 %fusion = bf16[1,512,6144]{1,2,0:T(8,128)(2,1)} fusion(bf16[1024,6144]{0,1:T(8,128)(2,1)} %bitcast.10, bf16[1,1024,512]{2,1,0:T(8,128)(2,1)S(1)} %copy-done), kind=kOutput, calls=%fused_computation.2 | convolution fusion | flops 6445596672 | bytes 19922944 | tf_op jit(solution)/shard_map/dot_general | solution.py:48
  397.2 8.6 %copy.58 = bf16[1,512,6144]{2,1,0:T(8,128)(2,1)} copy(bf16[1,512,6144]{1,2,0:T(8,128)(2,1)} %fusion) | data formatting | bytes 12582912
  (4 shorter events, 0.1 us)
Async XLA Ops:
  7.2 1.2 copy-start
  7.2 111.7 %reduce-scatter.2.cloned.1.call-start = ((), (), s32[]{:S(2)}) async-start(), calls=%async_computation.3 | async-start | bytes 13369344 | tf_op jit(solution)/shard_map/reduce_scatter | solution.py:29
  20.7 0.7 copy-start.2
  20.7 2.2 copy-start.3
  20.7 2.3 copy-start.1
  20.7 189.5 %all-gather.2.cloned.1.call-start = ((), (), s32[]{:S(2)}) async-start(), calls=%async_computation.4 | async-start | bytes 13369344 | tf_op jit(solution)/shard_map/all_gather | solution.py:42
  162.9 63.8 %all-to-all-start = ((bf16[8,2,24576]{2,1,0:T(2,128)(2,1)}), bf16[8,2,24576]{2,1,0:T(2,128)(2,1)S(1)}, u32[]{:S(2)}, u32[]{:S(2)}) async-start(bf16[8,2,24576]{2,1,0:T(2,128)(2,1)} %reshape.59), calls=%async_computation.1 | async-start | bytes 1572864 | tf_op jit(solution)/shard_map/all_to_all | solution.py:36
  226.7 144.9 %all-to-all-start.1 = ((bf16[8,1024,768]{1,2,0:T(8,128)(2,1)}), bf16[8,1024,768]{1,2,0:T(8,128)(2,1)}, u32[]{:S(2)}, u32[]{:S(2)}) async-start(bf16[8,1024,768]{1,2,0:T(8,128)(2,1)} %copy.57), calls=%async_computation.2 | async-start | bytes 25165824 | tf_op jit(solution)/shard_map/all_to_all | solution.py:43
Sparse Core Ops, SparseCore 0:
  20.8 98.0 reduce-scatter.1
  121.0 89.1 all-gather.1
where the time goes:
time: 414 us; the launch traced here: 413 us
  waiting for transfers between devices  263 us (64%)
  local copies, waits for them, and re-layouts  49 us (12%)
  matrix products  39.8 us (10%)
  other arithmetic  35.1 us (8%)
  between operations  14.1 us (3%)
  starting transfers between devices  11.7 us (3%)
    all_to_all x1, waiting for transfers between devices, body(): lax.all_to_all(shards, 'expert', split_axis=0, concat_axis=2, tiled=True)  127 us
    reduce_scatter x1, waiting for transfers between devices, body(): lax.psum_scatter(jnp.dot(hidden_rows, weight, preferred_element_type=jnp....  93.8 us
    all_gather x1, waiting for transfers between devices, body(): shards = lax.all_gather(routed, 'dp', axis=1, tiled=True)  41.9 us
    unnamed x1, other arithmetic  34.3 us
    unnamed x14, local copies, waits for them, and re-layouts  17 us
    all_gather x1, local copies, waits for them, and re-layouts, body(): shards = lax.all_gather(routed, 'dp', axis=1, tiled=True)  16.5 us
    dot_general x1, matrix products, body(): lax.dot_general(hidden_rows, grad_rows, (((0,), (0,)), ((), ())), preferr...  13.1 us
    dot_general x1, matrix products, body(): lax.dot_general(grad_rows, weight, (((1,), (1,)), ((), ())), preferred_el...  12.4 us
  transfers between devices with their start and end apart: 4, of which 3 were waited for; matrix products, arithmetic and copies ran while one was open for 18% of the time, Pallas kernels for 0%

commit v1 on v0

--- a/solution.py
+++ b/solution.py
@@ -39,7 +39,9 @@
     mixed_out = mixed_out.astype(jnp.bfloat16)
     routed = jnp.dot(dispatch, grad_out.astype(jnp.float32), precision=highest).astype(jnp.bfloat16)
     routed = routed.reshape(experts, capacity, routed.shape[-1])
-    shards = lax.all_gather(routed, "dp", axis=1, tiled=True)
+    shards = jnp.concatenate(
+        lax.all_to_all(jnp.stack([routed] * lax.axis_size("dp")), "dp", 0, 0), axis=1
+    )
     gathered = lax.all_to_all(shards, "expert", split_axis=0, concat_axis=2, tiled=True)
     grad_rows = gathered[0]
     hidden_acc = lax.dot_general(

time: 414 us -> 481 us (1.16)
  blocking collectives: 0 us -> 330 us
  waiting for transfers between devices: 263 us -> 0.02 us
  starting transfers between devices: 11.7 us -> 4.72 us
  local copies, waits for them, and re-layouts: 49 us -> 55.9 us
    all_to_all x0 -> x2, blocking collectives: none -> 330 us  [the longest x1 185 us: body(): lax.all_to_all(jnp.stack([routed] * lax.axis_size('dp')), 'dp', 0, 0)]
    all_to_all x1 -> x0, waiting for transfers between devices: 127 us -> none  [body(): lax.all_to_all(shards, 'expert', split_axis=0, concat_axis=2, tiled=True)]
    reduce_scatter x1, waiting for transfers between devices: 93.8 us -> 0.01 us  [body(): lax.psum_scatter(jnp.dot(hidden_rows, weight, preferred_element_type=jnp....]
    all_gather x1 -> x0, waiting for transfers between devices: 41.9 us -> none  [body(): shards = lax.all_gather(routed, 'dp', axis=1, tiled=True)]
    all_to_all x0 -> x2, local copies, waits for them, and re-layouts: none -> 18.6 us  [the longest x1 16.6 us: body(): lax.all_to_all(shards, 'expert', split_axis=0, concat_axis=2, tiled=True)]
    all_gather x1 -> x0, local copies, waits for them, and re-layouts: 16.5 us -> none  [body(): shards = lax.all_gather(routed, 'dp', axis=1, tiled=True)]
    all_to_all x1 -> x0, starting transfers between devices: 6.24 us -> none  [body(): lax.all_to_all(shards, 'expert', split_axis=0, concat_axis=2, tiled=True)]
    another operation x1 -> x2, local copies, waits for them, and re-layouts: 0.01 us -> 6.05 us  [the longest x1 6.05 us: body(): jnp.stack([routed] * lax.axis_size('dp'))]
  transfers between devices with their start and end apart: 4 -> 2, of which waited for: 3 -> 0; matrix products, arithmetic and copies ran while one was open for 18% -> 13% of each run, Pallas kernels for 0% -> 0%
where the time goes in v1:
time: 481 us; the launch traced here: 479 us
  blocking collectives  330 us (69%)
  local copies, waits for them, and re-layouts  55.9 us (12%)
  matrix products  39.9 us (8%)
  other arithmetic  35.1 us (7%)
  between operations  14.1 us (3%)
    all_to_all x1, blocking collectives, body(): lax.all_to_all(jnp.stack([routed] * lax.axis_size('dp')), 'dp', 0, 0)  185 us
    all_to_all x1, blocking collectives, body(): lax.all_to_all(shards, 'expert', split_axis=0, concat_axis=2, tiled=True)  145 us
    unnamed x1, other arithmetic  34.3 us
    unnamed x16, local copies, waits for them, and re-layouts  17.1 us
    all_to_all x1, local copies, waits for them, and re-layouts, body(): lax.all_to_all(shards, 'expert', split_axis=0, concat_axis=2, tiled=True)  16.6 us
    dot_general x1, matrix products, body(): lax.dot_general(hidden_rows, grad_rows, (((0,), (0,)), ((), ())), preferr...  13.2 us
    dot_general x1, matrix products, body(): lax.dot_general(grad_rows, weight, (((1,), (1,)), ((), ())), preferred_el...  12.4 us
    dot_general x1, matrix products, body(): jnp.dot(hidden_rows, weight, preferred_element_type=jnp.float32)  12.3 us
  transfers between devices with their start and end apart: 2, of which 0 were waited for; matrix products, arithmetic and copies ran while one was open for 13% of the time, Pallas kernels for 0%

profile of v1, /device:TPU:1, one launch (start us, length us, event | category | flops | bytes accessed | tf_op | source)
XLA Modules:
  0.0 479.4 jit_solution(1901993128615095233)
XLA Ops:
  7.2 0.0 copy-start
  7.2 0.0 reduce-scatter.2.cloned.1.call-start
  7.2 1.2 copy-done
  8.4 12.3 %convolution_convert_fusion = bf16[1024,6144]{1,0:T(8,128)(2,1)} fusion(bf16[1,512,6144]{2,1,0:T(8,128)(2,1)} %param.6, bf16[1,1024,512]{2,1,0:T(8,128)(2,1)S(1)} %copy-done), kind=kOutput, calls=%fused_computation | convolution fusion | flops 6448742400 | bytes 19922944 | tf_op jit(solution)/shard_map/dot_general | solution.py:30
  20.7 0.0 copy-start.3
  20.7 0.0 copy-start.4
  20.7 0.0 copy-start.2
  20.7 0.0 reduce-scatter.2.cloned.1.call-update
  20.8 0.6 copy-done.3
  21.4 0.1 copy.50
  21.5 0.1 eq.44
  21.7 0.6 reduce-window.6
  22.3 0.2 slice_reduce_fusion
  22.5 0.1 eq.40
  22.7 0.1 fusion.13
  22.8 0.1 reduce_sum.21
  22.9 0.1 copy.52
  23.0 0.0 copy-done.4
  23.0 0.1 select_reduce_fusion
  23.1 0.0 copy-done.2
  23.1 0.8 convolution_convert_fusion.2
  23.8 6.0 %stack.3 = bf16[16,8,64,768]{3,2,1,0:T(8,128)(2,1)} broadcast(bf16[8,64,768]{2,1,0:T(8,128)(2,1)S(1)} %bitcast.60), dimensions={1,2,3} | broadcast | bytes 13369344 | tf_op jit(solution)/shard_map/stack | solution.py:43
  29.9 184.8 %all_to_all.35 = bf16[16,8,64,768]{3,2,1,0:T(8,128)(2,1)S(1)} all-to-all(bf16[16,8,64,768]{3,2,1,0:T(8,128)(2,1)} %stack.3), channel_id=1, replica_groups=mesh['dp'=16,'expert'=8] {'dp'}, dimensions={0} | all-to-all | bytes 25165824 | tf_op jit(solution)/shard_map/all_to_all | solution.py:43
  214.7 1.9 copy.56
  216.6 144.8 %all_to_all.36 = bf16[8,1024,768]{2,1,0:T(8,128)(2,1)} all-to-all(bf16[8,1024,768]{2,1,0:T(8,128)(2,1)S(1)} %bitcast.54), channel_id=1, replica_groups=mesh['dp'=16,'expert'=8] {'expert'}, dimensions={0} | all-to-all | bytes 25165824 | tf_op jit(solution)/shard_map/all_to_all | solution.py:45
  361.4 16.6 %copy.57 = bf16[1,1024,8,768]{1,3,2,0:T(8,128)(2,1)} copy(bf16[1,1024,8,768]{3,1,2,0:T(8,128)(2,1)} %bitcast.55) | data formatting | bytes 25165824 | tf_op jit(solution)/shard_map/all_to_all | solution.py:45
  378.0 13.2 %fusion = bf16[1,512,6144]{1,2,0:T(8,128)(2,1)} fusion(bf16[1024,6144]{0,1:T(8,128)(2,1)} %bitcast.56, bf16[1,1024,512]{2,1,0:T(8,128)(2,1)S(1)} %copy-done), kind=kOutput, calls=%fused_computation.2 | convolution fusion | flops 6445596672 | bytes 19922944 | tf_op jit(solution)/shard_map/dot_general | solution.py:50
  391.2 0.0 reduce-scatter.2.cloned.1.call-done
  391.2 7.2 %copy.53 = bf16[1,64,6144]{1,0,2:T(2,128)(2,1)} copy(bf16[1,64,6144]{2,1,0:T(8,128)(2,1)} %bitcast.64) | data formatting | bytes 1572864 | tf_op jit(solution)/shard_map/broadcast_in_dim | solution.py:35
  398.5 0.5 broadcast.38
  399.0 34.3 %reduce.2 = bf16[6144,64]{1,0:T(8,128)(2,1)S(1)} reduce(bf16[6144,1,64]{2,1,0:T(2,128)(2,1)} %bitcast.58, bf16[]{:T(256)} %broadcast.38), dimensions={1}, to_apply=%bitcast.45.reduce_sub_computation | reduce | bytes 1572866
  433.3 1.9 reshape.65
  435.2 4.7 all-to-all-start
  439.9 0.0 copy-start.1
  439.9 12.4 %fusion.7 = bf16[1,1024,512]{2,1,0:T(8,128)(2,1)} fusion(bf16[1024,6144]{0,1:T(8,128)(2,1)} %bitcast.57, bf16[1,512,6144]{2,1,0:T(8,128)(2,1)} %param.6), kind=kOutput, calls=%fused_computation.8 | convolution fusion | flops 6442975232 | bytes 19922944 | tf_op jit(solution)/shard_map/dot_general | solution.py:47
  452.3 8.6 %copy.58 = bf16[1,512,6144]{2,1,0:T(8,128)(2,1)} copy(bf16[1,512,6144]{1,2,0:T(8,128)(2,1)} %fusion) | data formatting | bytes 12582912
  460.9 0.0 all-to-all-done
  460.9 4.0 reshape.66
  464.9 6.0 %copy.54 = bf16[1,64,6144]{2,1,0:T(8,128)(2,1)S(1)} copy(bf16[1,64,6144]{1,0,2:T(2,128)(2,1)} %bitcast.59) | data formatting | bytes 1572864 | tf_op jit(solution)/shard_map/all_to_all | solution.py:36
  471.0 0.1 copy.59
  471.2 0.1 bitcast_bitcast_fusion
  471.2 0.1 copy.55
  471.4 1.2 convolution_convert_fusion.3
  472.6 0.0 copy-done.1
  (4 shorter events, 0.1 us)
Async XLA Ops:
  7.2 1.2 copy-start
  7.2 384.0 %reduce-scatter.2.cloned.1.call-start = ((), (), s32[]{:S(2)}) async-start(), calls=%async_computation.4 | async-start | bytes 13369344 | tf_op jit(solution)/shard_map/reduce_scatter | solution.py:29
  20.7 0.7 copy-start.3
  20.7 2.2 copy-start.4
  20.7 2.3 copy-start.2
  435.2 25.7 %all-to-all-start = ((bf16[8,2,24576]{2,1,0:T(2,128)(2,1)}), bf16[8,2,24576]{2,1,0:T(2,128)(2,1)S(1)}, u32[]{:S(2)}, u32[]{:S(2)}) async-start(bf16[8,2,24576]{2,1,0:T(2,128)(2,1)} %reshape.65), calls=%async_computation.1 | async-start | bytes 1572864 | tf_op jit(solution)/shard_map/all_to_all | solution.py:36
  439.9 32.7 %copy-start.1 = (bf16[1,1024,512]{2,1,0:T(8,128)(2,1)S(1)}, bf16[1,1024,512]{2,1,0:T(8,128)(2,1)}, u32[]{:S(2)}) copy-start(bf16[1,1024,512]{2,1,0:T(8,128)(2,1)} %param.5) | copy-start | bytes 3145732
Sparse Core Ops, SparseCore 0:
  20.9 229.3 reduce-scatter.1
